TPU v7x, 32 devices: a whole 2x2x4 slice. The times are simulated.
32 devices in a mesh: scan: 8 (over z, x), bin: 4 (over y, core).
Axes of the slice: x: 2, y: 2, z: 4, core: 2. Of those that a mesh axis runs over, the one named last changes fastest.
Arguments:
- tile_blocks: bfloat16 [64, 16, 256, 256], P('scan', 'bin'), may hold values from -0.25 to 0.25
- tile_pattern: int32 [2, 64], P(None, 'scan'), may hold values from 0 to 63, as said below
- tile_count: int32 [8], P('scan'), may hold values from 1 to 8, as said below
- initial_map: float32 [16, 4, 4096], P('bin', None, 'scan')
- measured: float32 [16, 4, 16384], P('bin', None, 'scan')
- step_size: float32 [1], replicated, may hold values from 0.06 to 0.1
- penalty: float32 [4096], P('scan'), may hold values from 40 to 200
Outputs:
- source_map: float32 [16, 4, 4096], P('bin', None, 'scan')
Inputs may be any that keep to these rules, and one draw needn't show every extreme that they name: `tile_pattern`: row 0 names a sensor block of 64; row 1 of slot s names one of the 2 scan tiles (s // 8) * 2 to (s // 8) * 2 + 1. Only the first tile_count[d] slots of index d of scan are live; in every draw some indices have all 8 slots live.
All inputs are finite; a program needn't handle non-finite values.
Results may differ from a plain program's by a relative error of at most 0.00074.
Values may be sent and summed in bfloat16 or wider, within the bound.
No kernel may reach another device: no remote copies, remote signals or barrier semaphores. Data moves between devices by JAX's collectives and lax.ppermute only.
A program may use at most 64 MiB of HBM per device.

v0:
```python
import functools

import jax
import jax.numpy as jnp
from jax import lax
from jax.experimental import pallas as pl
from jax.experimental.pallas import tpu as pltpu
from jax.sharding import PartitionSpec as P


ITERS = 2
BITS = 14
ROWS_AT = 128
PRODUCT_AT = 64
F32 = jnp.float32
BF16 = jnp.bfloat16
I32 = jnp.int32
I16 = jnp.int16


def partners(count, k):
    if count & (count - 1):
        return [(i, (i + k) % count) for i in range(count)]
    return [(i, i ^ k) for i in range(count)]


def vmem():
    return pl.BlockSpec(memory_space=pltpu.VMEM)


def smem():
    return pl.BlockSpec(memory_space=pltpu.SMEM)


def hbm():
    return pl.BlockSpec(memory_space=pltpu.HBM)


def in_hbm(value):
    return pltpu.with_memory_space_constraint(value, pltpu.HBM)


def taker(refs):
    refs = list(refs)

    def take(n):
        taken, refs[:] = refs[:n], refs[n:]
        return taken

    return take


class Info:
    def __init__(self, ref, slots):
        self.ref, self.slots = ref, slots

    @staticmethod
    def size(slots):
        return 3 * slots + 2

    def row(self, s):
        return self.ref[s]

    def col(self, s):
        return self.ref[self.slots + s]

    def first(self, s):
        return self.ref[2 * self.slots + s]

    def shared(self):
        return self.ref[3 * self.slots]

    def live(self):
        return self.ref[3 * self.slots + 1]

    def fill(self, pattern_ref, count_ref, columns):
        slots, live = self.slots, count_ref[0]
        rows = [pattern_ref[0, s] for s in range(slots)]
        flag = jnp.int32(0)
        for s in range(slots):
            first = jnp.int32(s)
            for t in range(s - 1, -1, -1):
                first = jnp.where((rows[t] == rows[s]) & (s < live), t, first)
            self.ref[s] = rows[s]
            self.ref[slots + s] = lax.rem(pattern_ref[1, s], columns)
            self.ref[2 * slots + s] = first
            flag = flag | (first < s).astype(I32)
        self.ref[3 * slots] = flag
        self.ref[3 * slots + 1] = live


def start_tiles(a_hbm, a_ref, sems, low, high):
    copies = [pltpu.make_async_copy(a_hbm.at[s], a_ref.at[s], sems.at[s]) for s in range(low, high)]
    for copy in copies:
        copy.start()
    return copies


def masked_rows(value, bins, snaps):
    row = lax.broadcasted_iota(I32, value.shape, 0) // snaps
    return [jnp.where(row == f, value, 0.0).astype(BF16) for f in range(bins)]


def encode(value):
    top = jnp.max(jnp.abs(value), axis=1, keepdims=True)
    power = jnp.clip(jnp.ceil(jnp.log2(jnp.maximum(top, 1e-30))), -100.0, 127.0)
    code = jnp.clip(jnp.round(value * jnp.exp2(BITS - power)), -32767.0, 32767.0)
    return code.astype(I32).astype(I16), power.astype(I32)


def decode(code, note, lane, at):
    power = jnp.sum(jnp.where(lane == at, note, 0.0), axis=1, keepdims=True)
    return code.astype(I32).astype(F32) * jnp.exp2(power - BITS)


def forward(value, snaps, info, waits, xm_ref, a_ref, c_ref):
    slots, bins, tile = a_ref.shape[0], a_ref.shape[1], a_ref.shape[-1]
    for f, part in enumerate(masked_rows(value, bins, snaps)):
        xm_ref[f] = part
    for s in range(slots):
        for copy in waits.get(s, ()):
            copy.wait()
        start = pl.multiple_of(info.col(s) * tile, tile)
        total = None
        for f in range(bins):
            part = lax.dot_general(
                xm_ref[f, :, pl.ds(start, tile)],
                a_ref[s, f],
                (((1,), (1,)), ((), ())),
                preferred_element_type=F32,
            )
            total = part if total is None else total + part
        c_ref[s] = total

    @pl.when(info.shared() > 0)
    def _():
        for s in range(1, slots):
            first = info.first(s)

            @pl.when(first < s)
            def _():
                c_ref[first] += c_ref[s]


def start_kernel(coded, columns, count_ref, pattern_hbm, x_hbm, m_hbm, a_hbm, *refs):
    cur_ref, c_ref, out_ref, info_ref, pattern_ref, x_ref, m_ref, a_ref, xm_ref, small, sems = refs
    slots = a_ref.shape[0]
    bins, snaps = x_ref.shape[:2]
    loads = [
        pltpu.make_async_copy(source, target, small.at[i])
        for i, (source, target) in enumerate(
            [(pattern_hbm, pattern_ref), (x_hbm, x_ref), (m_hbm, m_ref)]
        )
    ]
    for load in loads:
        load.start()
    copies = start_tiles(a_hbm, a_ref, sems, 0, slots * 3 // 4)
    loads[0].wait()
    info = Info(info_ref, slots)
    info.fill(pattern_ref, count_ref, columns)
    loads[1].wait()
    value = jnp.concatenate([x_ref[f] for f in range(bins)], axis=0)
    cur_ref[...] = value
    copies += start_tiles(a_hbm, a_ref, sems, slots * 3 // 4, slots)
    waits = {0: copies[: slots * 3 // 4], slots * 3 // 4: copies[slots * 3 // 4 :]}
    loads[2].wait()
    lanes, tile = out_ref.shape[1:]
    if coded:
        own = out_ref.shape[0] - slots - 1
        lane = lax.broadcasted_iota(I32, (lanes, tile), 1)
        note = jnp.full((lanes, tile), -1, I32)
        for b in range(own):
            code, power = encode(
                jnp.concatenate([m_ref[f, :, b * tile : (b + 1) * tile] for f in range(bins)], axis=0)
            )
            out_ref[b] = code
            note = jnp.where(lane == b, power, note)
        for s in range(slots):
            keep = (s < info.live()) & (info.first(s) == s)
            note = jnp.where((lane == ROWS_AT + s) & keep, info.row(s), note)
    forward(value, snaps, info, waits, xm_ref, a_ref, c_ref)
    for s in range(slots):
        if coded:
            code, power = encode(c_ref[s])
            out_ref[own + s] = code
            note = jnp.where(lane == PRODUCT_AT + s, power, note)
        else:
            out_ref[s] = c_ref[s].astype(BF16)
    if coded:
        out_ref[own + slots] = note.astype(I16)


def shrink(moved, energies, step, penalty):
    energy = energies[0]
    for other in energies[1:]:
        energy = energy + other
    return moved * jnp.maximum(0.0, 1.0 - step * penalty / jnp.sqrt(energy + 1e-6))


def next_kernel(groups, snaps, *refs):
    take = taker(refs)
    info_ref, step_ref, moved_ref = take(3)
    energy_refs = take(groups)
    penalty_ref, a_ref, cur_ref, c_ref, out_ref, xm_ref = take(6)
    slots = a_ref.shape[0]
    value = shrink(moved_ref[...], [e[...] for e in energy_refs], step_ref[0], penalty_ref[...])
    cur_ref[...] = value
    forward(value, snaps, Info(info_ref, slots), {}, xm_ref, a_ref, c_ref)
    for s in range(slots):
        out_ref[s] = c_ref[s].astype(BF16)


def last_kernel(groups, snaps, *refs):
    take = taker(refs)
    step_ref, moved_ref = take(2)
    energy_refs = take(groups)
    penalty_ref, out_ref = take(2)
    value = shrink(moved_ref[...], [e[...] for e in energy_refs], step_ref[0], penalty_ref[...])
    for f in range(out_ref.shape[0]):
        out_ref[f] = value[f * snaps : (f + 1) * snaps]


def find_common(info, steps, slots, me, rows, order_ref, table, sem, entries_ref):
    sources = rows.shape[0]
    other = lax.broadcasted_iota(I32, rows.shape, 0)
    if steps is not None:
        far = jnp.zeros(rows.shape, I32)
        for i, k in enumerate(steps):
            far = jnp.where(other == i, k, far)
        other = far ^ me
    found = jnp.full(rows.shape, -1, I32)
    for s in range(slots):
        row = jnp.where((s < info.live()) & (info.first(s) == s), info.row(s), -2)
        found = jnp.where(rows == row, s, found)
    order_ref[...] = jnp.where(other == me, -1, found)
    copy = pltpu.make_async_copy(order_ref, table, sem)
    copy.start()

    def finish():
        copy.wait()

        def one(k, number):
            entries_ref[k] = number
            for t in range(slots):
                slot = table[k, t]
                entries_ref[number] = (t if steps is not None else k * slots + t) * 64 + slot
                number = number + (slot >= 0).astype(I32)
            return number

        entries_ref[sources] = lax.fori_loop(0, sources, one, jnp.int32(sources + 1))

    return finish


def gradient(info, columns, snaps, a_ref, r_ref):
    slots, bins, tile = a_ref.shape[0], a_ref.shape[1], a_ref.shape[-1]
    sums = [jnp.zeros((bins * snaps, tile), F32) for _ in range(columns)]
    for s in range(slots):
        value = jnp.where(s < info.live(), r_ref[info.first(s)], 0.0)
        lhs = jnp.concatenate(masked_rows(value, bins, snaps), axis=1)
        part = jnp.dot(lhs, a_ref[s].reshape(bins * tile, tile), preferred_element_type=F32)
        sums = [total + jnp.where(info.col(s) == i, part, 0.0) for i, total in enumerate(sums)]
    return jnp.concatenate(sums, axis=1)


def finish_step(cur_ref, step_ref, grad, moved_ref, energy_ref):
    moved = cur_ref[...] - step_ref[0] * grad
    moved_ref[...] = moved
    energy_ref[...] = jnp.sum(moved * moved, axis=0, keepdims=True)


def take_in(steps, refs, info, me, rows_ref, order_ref, table, sem, entries_ref, sel_ref, r_ref):
    slots = r_ref.shape[0]
    last = refs[0].shape[0] - 1
    own = last - slots
    for i, ref in enumerate(refs):
        rows_ref[i : i + 1] = ref[last, 0:1, ROWS_AT : ROWS_AT + 128].astype(I32)
    finish = find_common(info, steps, slots, me, rows_ref[...], order_ref, table, sem, entries_ref)
    lane = lax.broadcasted_iota(I32, refs[0].shape[1:], 1)
    homes = [lax.bitwise_xor(me, lax.div(info.row(s), own)) for s in range(slots)]
    for k, ref in zip(steps, refs):
        some = homes[0] == k
        for home in homes[1:]:
            some = some | (home == k)

        @pl.when(some)
        def _(k=k, ref=ref):
            note = ref[last].astype(I32).astype(F32)
            for s in range(slots):

                @pl.when(homes[s] == k)
                def _(s=s):
                    at = lax.rem(info.row(s), own)
                    value = decode(ref[at], note, lane, at)
                    sel_ref[s] = value
                    r_ref[s] -= value

    finish()
    for i, ref in enumerate(refs):

        def add(j, _, ref=ref):
            at, slot = lax.shift_right_logical(entries_ref[j], 6), entries_ref[j] & 63
            note = ref[last].astype(I32).astype(F32)
            r_ref[slot] += decode(ref[own + at], note, lane, PRODUCT_AT + at)
            return 0

        lax.fori_loop(entries_ref[i], entries_ref[i + 1], add, 0)


def early_kernel(coded, steps, *refs):
    take = taker(refs)
    info_ref, me_ref, c_ref, a_hbm = take(4)
    arrived = take(len(steps) if coded else 3)
    r_ref, sel_ref, a_ref, entries_ref, rows_ref, order_ref, table, sem, sems = take(9)
    slots = a_ref.shape[0]
    info = Info(info_ref, slots)
    me = me_ref[0]
    copies = start_tiles(a_hbm, a_ref, sems, 0, slots)
    r_ref[...] = c_ref[...]
    sel_ref[...] = jnp.zeros_like(sel_ref)
    if coded:
        take_in(steps, arrived, info, me, rows_ref, order_ref, table, sem, entries_ref, sel_ref, r_ref)
    else:
        full_ref, table_ref, recv_ref = arrived
        finish = find_common(info, None, slots, me, table_ref[...], order_ref, table, sem, entries_ref)
        for s in range(slots):
            sel_ref[s] = full_ref[info.row(s)]
            r_ref[s] -= sel_ref[s]
        finish()
        add_blocks(entries_ref, 0, table_ref.shape[0], recv_ref, r_ref)
    for copy in copies:
        copy.wait()


def late_kernel(steps, snaps, *refs):
    take = taker(refs)
    info_ref, step_ref, me_ref, part_ref, some_ref, cur_ref, a_ref = take(7)
    arrived = take(len(steps))
    moved_ref, energy_ref, sel_ref, entries_ref, r_ref = take(5)
    slots, tile = a_ref.shape[0], a_ref.shape[-1]
    info = Info(info_ref, slots)
    r_ref[...] = part_ref[...]
    sel_ref[...] = some_ref[...]
    if steps:
        rows_ref, order_ref, table, sem = take(4)
        take_in(steps, arrived, info, me_ref[0], rows_ref, order_ref, table, sem, entries_ref, sel_ref, r_ref)
    else:
        entries_ref[0] = 1
    grad = gradient(info, cur_ref.shape[1] // tile, snaps, a_ref, r_ref)
    finish_step(cur_ref, step_ref, grad, moved_ref, energy_ref)


def add_blocks(entries_ref, low, high, ref, r_ref):
    def add(i, _):
        at, slot = lax.shift_right_logical(entries_ref[i], 6), entries_ref[i] & 63
        r_ref[slot] += ref[at].astype(F32)
        return 0

    lax.fori_loop(entries_ref[low], entries_ref[high], add, 0)


def back_kernel(coded, steps, snaps, *refs):
    take = taker(refs)
    info_ref, step_ref = take(2)
    entry_refs = take(len(steps))
    c_ref, cur_ref, sel_ref, a_ref = take(4)
    arrived = dict(enumerate(take(max(k for part in steps for k in part) if coded else 1), 1))
    moved_ref, energy_ref, r_ref = take(3)
    slots, tile = a_ref.shape[0], a_ref.shape[-1]
    info = Info(info_ref, slots)
    for s in range(slots):
        r_ref[s] = c_ref[s] - sel_ref[s]
    if coded:
        for entries_ref, part in zip(entry_refs, steps):
            for i, k in enumerate(part):
                if k:
                    add_blocks(entries_ref, i, i + 1, arrived[k], r_ref)
    else:
        add_blocks(entry_refs[0], 0, arrived[1].shape[0] // slots, arrived[1], r_ref)
    grad = gradient(info, cur_ref.shape[1] // tile, snaps, a_ref, r_ref)
    finish_step(cur_ref, step_ref, grad, moved_ref, energy_ref)


def body(count, groups, tile_blocks, tile_pattern, tile_count, initial_map, measured, step_size, penalty):
    slots, bins, tile, _ = tile_blocks.shape
    snaps, points = initial_map.shape[1:]
    lanes = bins * snaps
    sensors_dev = measured.shape[2]
    blocks = sensors_dev * count // tile
    columns = points // tile
    own = sensors_dev // tile
    me = lax.axis_index("scan").astype(I32)[None]
    shape = jax.ShapeDtypeStruct
    grant = pltpu.CompilerParams(vmem_limit_bytes=20 << 20)
    coded = (
        count <= 8
        and count & (count - 1) == 0
        and sensors_dev % tile == 0
        and own <= PRODUCT_AT
        and slots < 64
        and tile >= ROWS_AT + 128
    )
    map_shape = shape((lanes, points), F32)
    slot_shape = shape((slots, lanes, tile), F32)
    sent_shape = shape((slots, lanes, tile), BF16)
    tile_shape = shape(tile_blocks.shape, BF16)
    masked = pltpu.VMEM((bins, lanes, points), BF16)
    tile_sems = pltpu.SemaphoreType.DMA((slots,))

    def swap(value, k):
        return lax.ppermute(value, "scan", [(i, i ^ k) for i in range(count)])

    def spread(value):
        if not coded:
            return [lax.all_gather(value, "scan", axis=0, tiled=True)]
        got = {}
        for k in range(2, count, 2):
            got[k] = swap(value, k)
        got[1] = swap(value, 1)
        for k in range(2, count, 2):
            got[k + 1] = swap(got[k], 1)
        return [got[k] for k in range(1, count)]

    current, contrib, sent, info = pl.pallas_call(
        functools.partial(start_kernel, coded, columns),
        out_shape=(
            map_shape,
            slot_shape,
            shape((own + slots + 1, lanes, tile), I16) if coded else sent_shape,
            shape((Info.size(slots),), I32),
        ),
        in_specs=[smem()] + [hbm()] * 4,
        out_specs=(vmem(), vmem(), vmem(), smem()),
        scratch_shapes=[
            pltpu.SMEM(tile_pattern.shape, I32),
            pltpu.VMEM(initial_map.shape, F32),
            pltpu.VMEM(measured.shape, F32),
            pltpu.VMEM(tile_blocks.shape, BF16),
            masked,
            pltpu.SemaphoreType.DMA((3,)),
            tile_sems,
        ],
        compiler_params=grant,
    )(tile_count, in_hbm(tile_pattern), in_hbm(initial_map), in_hbm(measured), in_hbm(tile_blocks))

    late = list(range(5, count, 2)) if coded else []
    early = [k for k in range(count) if k not in late] if coded else []
    if coded:
        given = [sent] + spread(sent)
        ready, waiting = [given[k] for k in early], [given[k] for k in late]
    else:
        full = lax.all_gather(measured, "scan", axis=2, tiled=True)
        order = jnp.arange(slots, dtype=I32)
        keep = (order < tile_count[0]) & (info[2 * slots : 3 * slots] == order)
        rows = jnp.pad(jnp.where(keep, tile_pattern[0], -1), (0, 128 - slots), constant_values=-1)
        ready = [
            full.reshape(lanes, blocks, tile).transpose(1, 0, 2),
            lax.all_gather(rows[None], "scan", axis=0, tiled=True),
        ] + spread(sent)
        waiting = []

    def plan_scratch(sources):
        return [
            pltpu.VMEM((sources, 128), I32),
            pltpu.VMEM((sources, 128), I32),
            pltpu.SMEM((sources, 128), I32),
            pltpu.SemaphoreType.DMA,
        ]

    def entries_shape(sources):
        return shape((sources + 2 + sources * slots,), I32)

    pen = penalty.reshape(1, points)
    energy_shape = shape((1, points), F32)
    for iteration in range(ITERS):
        if iteration == 0:
            sources = len(early) if coded else count
            partial, some, held, entries = pl.pallas_call(
                functools.partial(early_kernel, coded, early),
                out_shape=(slot_shape, slot_shape, tile_shape, entries_shape(sources)),
                in_specs=[smem()] * 2 + [vmem(), hbm()] + [vmem()] * len(ready),
                out_specs=(vmem(),) * 3 + (smem(),),
                scratch_shapes=plan_scratch(sources) + [tile_sems],
                compiler_params=grant,
            )(info, me, contrib, in_hbm(tile_blocks), *ready)
            moved, energy, chosen, more = pl.pallas_call(
                functools.partial(late_kernel, late, snaps),
                out_shape=(map_shape, energy_shape, slot_shape, entries_shape(len(late))),
                in_specs=[smem()] * 3 + [vmem()] * (4 + len(waiting)),
                out_specs=(vmem(),) * 3 + (smem(),),
                scratch_shapes=[pltpu.VMEM(slot_shape.shape, F32)] + (plan_scratch(len(late)) if late else []),
                compiler_params=grant,
            )(info, step_size, me, partial, some, current, held, *waiting)
        else:
            received = spread(sent)
            moved, energy = pl.pallas_call(
                functools.partial(back_kernel, coded, (early, late), snaps),
                out_shape=(map_shape, energy_shape),
                in_specs=[smem()] * 4 + [vmem()] * (4 + len(received)),
                out_specs=(vmem(),) * 2,
                scratch_shapes=[pltpu.VMEM(slot_shape.shape, F32)],
                compiler_params=grant,
            )(info, step_size, entries, more, contrib, current, chosen, held, *received)
        energies = [energy] + [
            lax.ppermute(energy, "bin", partners(groups, k))
            for k in range(1, groups)
        ]
        if iteration < ITERS - 1:
            current, contrib, sent = pl.pallas_call(
                functools.partial(next_kernel, groups, snaps),
                out_shape=(map_shape, slot_shape, sent_shape),
                in_specs=[smem()] * 2 + [vmem()] * (3 + groups),
                out_specs=(vmem(),) * 3,
                scratch_shapes=[masked],
                compiler_params=grant,
            )(info, step_size, moved, *energies, pen, held)
    return pl.pallas_call(
        functools.partial(last_kernel, groups, snaps),
        out_shape=shape(initial_map.shape, F32),
        in_specs=[smem()] + [vmem()] * (2 + groups),
        out_specs=vmem(),
        compiler_params=grant,
    )(step_size, moved, *energies, pen)


def solution(mesh):
    in_specs = (
        P("scan", "bin", None, None),
        P(None, "scan"),
        P("scan"),
        P("bin", None, "scan"),
        P("bin", None, "scan"),
        P(),
        P("scan"),
    )
    count = mesh.shape["scan"]

    def run(*args):
        return body(count, mesh.shape["bin"], *args)

    return jax.shard_map(run, mesh=mesh, in_specs=in_specs, out_specs=P("bin", None, "scan"), check_vma=False)
```

profile of v0, /device:TPU:0, one launch (start us, length us, event | category | flops | bytes accessed | tf_op | source)
XLA Modules:
  0.0 57.1 jit_solution(13967366978907937359)
XLA Ops:
  0.7 3.9 %shard_map.73 = (f32[16,512]{1,0:T(8,128)S(1)}, f32[8,16,256]{2,1,0:T(8,128)S(1)}, s16[17,16,256]{2,1,0:T(8,128)(2,1)S(1)}, s32[26]{0:T(128)S(1)}) custom-call(s32[1]{0:T(128)S(6)} %copy.8.count_ref, s32[2,8]{1,0:T(2,128)} %pattern_hbm.1, f32[4,4,512]{2,1,0:T(4,128)} %x_hbm.1, f32[4,4,2048]{2,1,0:T(4,128)} %m_hbm.1, bf16[8,4,256,256]{3,2,1,0:T(8,128)(2,1)} %refs_3_.1), custom_call_target="tpu_custom_call" | custom-call | tf_op jit(solution)/shard_map/pallas_call | solution.py:424
  4.6 3.1 %collective-permute-start.1 = (s16[17,16,256]{2,1,0:T(8,128)(2,1)S(1)}, s16[17,16,256]{2,1,0:T(8,128)(2,1)S(1)}, u32[]{:S(2)}, u32[]{:S(2)}) collective-permute-start(s16[17,16,256]{2,1,0:T(8,128)(2,1)S(1)} %get-tuple-element.24.refs_4_), channel_id=1, source_target_pairs={{0,8},{4,12},{8,0},{12,4},{16,24},{20,28},{24,16},{28,20},{1,9},{5... | collective-permute-start | bytes 417800 | tf_op jit(solution)/shard_map/ppermute | solution.py:411
  7.7 2.6 %collective-permute-start.3 = (s16[17,16,256]{2,1,0:T(8,128)(2,1)S(1)}, s16[17,16,256]{2,1,0:T(8,128)(2,1)S(1)}, u32[]{:S(2)}, u32[]{:S(2)}) collective-permute-start(s16[17,16,256]{2,1,0:T(8,128)(2,1)S(1)} %get-tuple-element.24.refs_4_), channel_id=1, source_target_pairs={{0,16},{4,20},{8,24},{12,28},{16,0},{20,4},{24,8},{28,12},{1,17},{... | collective-permute-start | bytes 417800 | tf_op jit(solution)/shard_map/ppermute | solution.py:411
  10.3 1.7 %collective-permute-start = (s16[17,16,256]{2,1,0:T(8,128)(2,1)S(1)}, s16[17,16,256]{2,1,0:T(8,128)(2,1)S(1)}, u32[]{:S(2)}, u32[]{:S(2)}) collective-permute-start(s16[17,16,256]{2,1,0:T(8,128)(2,1)S(1)} %get-tuple-element.24.refs_4_), channel_id=1, source_target_pairs={{0,4},{4,0},{8,12},{12,8},{16,20},{20,16},{24,28},{28,24},{1,5},{5... | collective-permute-start | bytes 417800 | tf_op jit(solution)/shard_map/ppermute | solution.py:411
  12.0 1.2 %collective-permute-done.1.refs_6_ = s16[17,16,256]{2,1,0:T(8,128)(2,1)S(1)} collective-permute-done((s16[17,16,256]{2,1,0:T(8,128)(2,1)S(1)}, s16[17,16,256]{2,1,0:T(8,128)(2,1)S(1)}, u32[]{:S(2)}, u32[]{:S(2)}) %collective-permute-start.1) | collective-permute-done | bytes 139296 | tf_op jit(solution)/shard_map/ppermute | solution.py:411
  13.2 1.7 %collective-permute-start.2 = (s16[17,16,256]{2,1,0:T(8,128)(2,1)S(1)}, s16[17,16,256]{2,1,0:T(8,128)(2,1)S(1)}, u32[]{:S(2)}, u32[]{:S(2)}) collective-permute-start(s16[17,16,256]{2,1,0:T(8,128)(2,1)S(1)} %collective-permute-done.1.refs_6_), channel_id=1, source_target_pairs={{0,4},{4,0},{8,12},{12,8},{16,20},{20,16},{24,28},{28,24},{1,5},{5... | collective-permute-start | bytes 417800 | tf_op jit(solution)/shard_map/ppermute | solution.py:411
  14.9 6.2 %collective-permute-done.3.refs_8_ = s16[17,16,256]{2,1,0:T(8,128)(2,1)S(1)} collective-permute-done((s16[17,16,256]{2,1,0:T(8,128)(2,1)S(1)}, s16[17,16,256]{2,1,0:T(8,128)(2,1)S(1)}, u32[]{:S(2)}, u32[]{:S(2)}) %collective-permute-start.3) | collective-permute-done | bytes 139296 | tf_op jit(solution)/shard_map/ppermute | solution.py:411
  21.1 1.5 %collective-permute-start.5 = (s16[17,16,256]{2,1,0:T(8,128)(2,1)S(1)}, s16[17,16,256]{2,1,0:T(8,128)(2,1)S(1)}, u32[]{:S(2)}, u32[]{:S(2)}) collective-permute-start(s16[17,16,256]{2,1,0:T(8,128)(2,1)S(1)} %collective-permute-done.3.refs_8_), channel_id=1, source_target_pairs={{0,4},{4,0},{8,12},{12,8},{16,20},{20,16},{24,28},{28,24},{1,5},{5... | collective-permute-start | bytes 417800 | tf_op jit(solution)/shard_map/ppermute | solution.py:411
  23.8 3.4 %shard_map.74 = (f32[8,16,256]{2,1,0:T(8,128)S(1)}, f32[8,16,256]{2,1,0:T(8,128)S(1)}, bf16[8,4,256,256]{3,2,1,0:T(8,128)(2,1)S(1)}, s32[56]{0:T(128)S(1)}) custom-call(s32[26]{0:T(128)S(1)} %get-tuple-element.22.refs_0_, s32[1]{0:T(128)} %bitcast.refs_1_.refs_2_, f32[8,16,256]{2,1,0:T(8,128)S(1)} %get-tuple-element.23.refs_2_, ...), custom_call_target="tpu_custom_call" | custom-call | tf_op jit(solution)/shard_map/pallas_call | solution.py:478
  27.6 2.1 %shard_map.75 = (f32[16,512]{1,0:T(8,128)S(1)}, f32[1,512]{1,0:T(1,128)S(1)}, f32[8,16,256]{2,1,0:T(8,128)S(1)}, s32[20]{0:T(128)S(1)}) custom-call(s32[26]{0:T(128)S(1)} %get-tuple-element.22.refs_0_, f32[1]{0:T(128)S(6)} %copy.9.refs_1_.refs_0_, s32[1]{0:T(128)} %bitcast.refs_1_.refs_2_, f32[8,16,256]{2,1,0:T(8,128)S(1)} %get-tuple-element.26.refs_3_, ...), custom_call_target="tpu_custom_call" | custom-call | tf_op jit(solution)/shard_map/pallas_call | solution.py:486
  29.9 1.6 %collective-permute-start.8 = (f32[1,512]{1,0:T(1,128)S(1)}, f32[1,512]{1,0:T(1,128)S(1)}, u32[]{:S(2)}, u32[]{:S(2)}) collective-permute-start(f32[1,512]{1,0:T(1,128)S(1)} %get-tuple-element.32.refs_3_), channel_id=1, source_target_pairs={{0,2},{1,3},{2,0},{3,1},{4,6},{5,7},{6,4},{7,5},{8,10},{9,11},{10,... | collective-permute-start | bytes 6152 | tf_op jit(solution)/shard_map/ppermute | solution.py:505
  31.7 1.8 %collective-permute-done.8.refs_5_ = f32[1,512]{1,0:T(1,128)S(1)} collective-permute-done((f32[1,512]{1,0:T(1,128)S(1)}, f32[1,512]{1,0:T(1,128)S(1)}, u32[]{:S(2)}, u32[]{:S(2)}) %collective-permute-start.8) | collective-permute-done | bytes 2080 | tf_op jit(solution)/shard_map/ppermute | solution.py:505
  34.5 1.7 %shard_map.76 = (f32[16,512]{1,0:T(8,128)S(1)}, f32[8,16,256]{2,1,0:T(8,128)S(1)}, bf16[8,16,256]{2,1,0:T(8,128)(2,1)S(1)}) custom-call(s32[26]{0:T(128)S(1)} %get-tuple-element.22.refs_0_, f32[1]{0:T(128)S(6)} %copy.9.refs_1_.refs_0_, f32[16,512]{1,0:T(8,128)S(1)} %get-tuple-element.31.refs_2_, f32[1,512]{1,0:T(1,128)S(1)} %get-tuple-element.32.refs_3_, ...), custom_call_target="tpu_custom_call" | custom-call | tf_op jit(solution)/shard_map/pallas_call | solution.py:509
  36.2 1.4 %collective-permute-start.11 = (bf16[8,16,256]{2,1,0:T(8,128)(2,1)S(1)}, bf16[8,16,256]{2,1,0:T(8,128)(2,1)S(1)}, u32[]{:S(2)}, u32[]{:S(2)}) collective-permute-start(bf16[8,16,256]{2,1,0:T(8,128)(2,1)S(1)} %get-tuple-element.36), channel_id=1, source_target_pairs={{0,8},{4,12},{8,0},{12,4},{16,24},{20,28},{24,16},{28,20},{1,9},{5... | collective-permute-start | bytes 196616 | tf_op jit(solution)/shard_map/ppermute | solution.py:411
  37.6 1.7 %collective-permute-start.13 = (bf16[8,16,256]{2,1,0:T(8,128)(2,1)S(1)}, bf16[8,16,256]{2,1,0:T(8,128)(2,1)S(1)}, u32[]{:S(2)}, u32[]{:S(2)}) collective-permute-start(bf16[8,16,256]{2,1,0:T(8,128)(2,1)S(1)} %get-tuple-element.36), channel_id=1, source_target_pairs={{0,16},{4,20},{8,24},{12,28},{16,0},{20,4},{24,8},{28,12},{1,17},{... | collective-permute-start | bytes 196616 | tf_op jit(solution)/shard_map/ppermute | solution.py:411
  39.3 1.3 %collective-permute-start.15 = (bf16[8,16,256]{2,1,0:T(8,128)(2,1)S(1)}, bf16[8,16,256]{2,1,0:T(8,128)(2,1)S(1)}, u32[]{:S(2)}, u32[]{:S(2)}) collective-permute-start(bf16[8,16,256]{2,1,0:T(8,128)(2,1)S(1)} %get-tuple-element.36), channel_id=1, source_target_pairs={{0,24},{4,28},{8,16},{12,20},{16,8},{20,12},{24,0},{28,4},{1,25},{... | collective-permute-start | bytes 196616 | tf_op jit(solution)/shard_map/ppermute | solution.py:411
  40.7 1.6 %collective-permute-start.10 = (bf16[8,16,256]{2,1,0:T(8,128)(2,1)S(1)}, bf16[8,16,256]{2,1,0:T(8,128)(2,1)S(1)}, u32[]{:S(2)}, u32[]{:S(2)}) collective-permute-start(bf16[8,16,256]{2,1,0:T(8,128)(2,1)S(1)} %get-tuple-element.36), channel_id=1, source_target_pairs={{0,4},{4,0},{8,12},{12,8},{16,20},{20,16},{24,28},{28,24},{1,5},{5... | collective-permute-start | bytes 196616 | tf_op jit(solution)/shard_map/ppermute | solution.py:411
  42.7 3.1 %collective-permute-done.13.refs_11_ = bf16[8,16,256]{2,1,0:T(8,128)(2,1)S(1)} collective-permute-done((bf16[8,16,256]{2,1,0:T(8,128)(2,1)S(1)}, bf16[8,16,256]{2,1,0:T(8,128)(2,1)S(1)}, u32[]{:S(2)}, u32[]{:S(2)}) %collective-permute-start.13) | collective-permute-done | bytes 65568 | tf_op jit(solution)/shard_map/ppermute | solution.py:411
  45.8 1.3 %collective-permute-start.14 = (bf16[8,16,256]{2,1,0:T(8,128)(2,1)S(1)}, bf16[8,16,256]{2,1,0:T(8,128)(2,1)S(1)}, u32[]{:S(2)}, u32[]{:S(2)}) collective-permute-start(bf16[8,16,256]{2,1,0:T(8,128)(2,1)S(1)} %collective-permute-done.13.refs_11_), channel_id=1, source_target_pairs={{0,4},{4,0},{8,12},{12,8},{16,20},{20,16},{24,28},{28,24},{1,5},{5... | collective-permute-start | bytes 196616 | tf_op jit(solution)/shard_map/ppermute | solution.py:411
  47.9 2.2 %collective-permute-done.14.refs_12_ = bf16[8,16,256]{2,1,0:T(8,128)(2,1)S(1)} collective-permute-done((bf16[8,16,256]{2,1,0:T(8,128)(2,1)S(1)}, bf16[8,16,256]{2,1,0:T(8,128)(2,1)S(1)}, u32[]{:S(2)}, u32[]{:S(2)}) %collective-permute-start.14) | collective-permute-done | bytes 65568 | tf_op jit(solution)/shard_map/ppermute | solution.py:411
  50.1 1.3 %collective-permute-done.16.refs_14_ = bf16[8,16,256]{2,1,0:T(8,128)(2,1)S(1)} collective-permute-done((bf16[8,16,256]{2,1,0:T(8,128)(2,1)S(1)}, bf16[8,16,256]{2,1,0:T(8,128)(2,1)S(1)}, u32[]{:S(2)}, u32[]{:S(2)}) %collective-permute-start.16) | collective-permute-done | bytes 65568 | tf_op jit(solution)/shard_map/ppermute | solution.py:411
  51.4 1.3 %shard_map.77 = (f32[16,512]{1,0:T(8,128)S(1)}, f32[1,512]{1,0:T(1,128)S(1)}) custom-call(s32[26]{0:T(128)S(1)} %get-tuple-element.22.refs_0_, f32[1]{0:T(128)S(6)} %copy.9.refs_1_.refs_0_, s32[56]{0:T(128)S(1)} %get-tuple-element.25.refs_2_, s32[20]{0:T(128)S(1)} %get-tuple-element.30.refs_3_, f32[8,16,256]{2,1,0:T(8,128)S(1)} %get-tuple-element.33.refs_4_, ...), custom_call_target="tpu_custom_call" | custom-call | tf_op jit(solution)/shard_map/pallas_call | solution.py:496
  53.4 1.2 %collective-permute-start.19 = (f32[1,512]{1,0:T(1,128)S(1)}, f32[1,512]{1,0:T(1,128)S(1)}, u32[]{:S(2)}, u32[]{:S(2)}) collective-permute-start(f32[1,512]{1,0:T(1,128)S(1)} %get-tuple-element.38.refs_2_), channel_id=1, source_target_pairs={{0,3},{1,2},{2,1},{3,0},{4,7},{5,6},{6,5},{7,4},{8,11},{9,10},{10,... | collective-permute-start | bytes 6152 | tf_op jit(solution)/shard_map/ppermute | solution.py:505
  54.6 1.8 %collective-permute-done.18.refs_4_ = f32[1,512]{1,0:T(1,128)S(1)} collective-permute-done((f32[1,512]{1,0:T(1,128)S(1)}, f32[1,512]{1,0:T(1,128)S(1)}, u32[]{:S(2)}, u32[]{:S(2)}) %collective-permute-start.18) | collective-permute-done | bytes 2080 | tf_op jit(solution)/shard_map/ppermute | solution.py:505
  (24 shorter events, 4.8 us)
Async XLA Ops:
  4.6 8.6 %collective-permute-start.1 = (s16[17,16,256]{2,1,0:T(8,128)(2,1)S(1)}, s16[17,16,256]{2,1,0:T(8,128)(2,1)S(1)}, u32[]{:S(2)}, u32[]{:S(2)}) collective-permute-start(s16[17,16,256]{2,1,0:T(8,128)(2,1)S(1)} %get-tuple-element.24.refs_4_), channel_id=1, source_target_pairs={{0,8},{4,12},{8,0},{12,4},{16,24},{20,28},{24,16},{28,20},{1,9},{5... | collective-permute-start | bytes 417800 | tf_op jit(solution)/shard_map/ppermute | solution.py:411
  7.7 13.4 %collective-permute-start.3 = (s16[17,16,256]{2,1,0:T(8,128)(2,1)S(1)}, s16[17,16,256]{2,1,0:T(8,128)(2,1)S(1)}, u32[]{:S(2)}, u32[]{:S(2)}) collective-permute-start(s16[17,16,256]{2,1,0:T(8,128)(2,1)S(1)} %get-tuple-element.24.refs_4_), channel_id=1, source_target_pairs={{0,16},{4,20},{8,24},{12,28},{16,0},{20,4},{24,8},{28,12},{1,17},{... | collective-permute-start | bytes 417800 | tf_op jit(solution)/shard_map/ppermute | solution.py:411
  10.3 12.3 %collective-permute-start.4 = (s16[17,16,256]{2,1,0:T(8,128)(2,1)S(1)}, s16[17,16,256]{2,1,0:T(8,128)(2,1)S(1)}, u32[]{:S(2)}, u32[]{:S(2)}) collective-permute-start(s16[17,16,256]{2,1,0:T(8,128)(2,1)S(1)} %get-tuple-element.24.refs_4_), channel_id=1, source_target_pairs={{0,24},{4,28},{8,16},{12,20},{16,8},{20,12},{24,0},{28,4},{1,25},{... | collective-permute-start | bytes 417800 | tf_op jit(solution)/shard_map/ppermute | solution.py:411
  10.3 13.5 %collective-permute-start = (s16[17,16,256]{2,1,0:T(8,128)(2,1)S(1)}, s16[17,16,256]{2,1,0:T(8,128)(2,1)S(1)}, u32[]{:S(2)}, u32[]{:S(2)}) collective-permute-start(s16[17,16,256]{2,1,0:T(8,128)(2,1)S(1)} %get-tuple-element.24.refs_4_), channel_id=1, source_target_pairs={{0,4},{4,0},{8,12},{12,8},{16,20},{20,16},{24,28},{28,24},{1,5},{5... | collective-permute-start | bytes 417800 | tf_op jit(solution)/shard_map/ppermute | solution.py:411
  13.2 10.6 %collective-permute-start.2 = (s16[17,16,256]{2,1,0:T(8,128)(2,1)S(1)}, s16[17,16,256]{2,1,0:T(8,128)(2,1)S(1)}, u32[]{:S(2)}, u32[]{:S(2)}) collective-permute-start(s16[17,16,256]{2,1,0:T(8,128)(2,1)S(1)} %collective-permute-done.1.refs_6_), channel_id=1, source_target_pairs={{0,4},{4,0},{8,12},{12,8},{16,20},{20,16},{24,28},{28,24},{1,5},{5... | collective-permute-start | bytes 417800 | tf_op jit(solution)/shard_map/ppermute | solution.py:411
  21.1 6.1 %collective-permute-start.5 = (s16[17,16,256]{2,1,0:T(8,128)(2,1)S(1)}, s16[17,16,256]{2,1,0:T(8,128)(2,1)S(1)}, u32[]{:S(2)}, u32[]{:S(2)}) collective-permute-start(s16[17,16,256]{2,1,0:T(8,128)(2,1)S(1)} %collective-permute-done.3.refs_8_), channel_id=1, source_target_pairs={{0,4},{4,0},{8,12},{12,8},{16,20},{20,16},{24,28},{28,24},{1,5},{5... | collective-permute-start | bytes 417800 | tf_op jit(solution)/shard_map/ppermute | solution.py:411
  22.6 5.1 %collective-permute-start.6 = (s16[17,16,256]{2,1,0:T(8,128)(2,1)S(1)}, s16[17,16,256]{2,1,0:T(8,128)(2,1)S(1)}, u32[]{:S(2)}, u32[]{:S(2)}) collective-permute-start(s16[17,16,256]{2,1,0:T(8,128)(2,1)S(1)} %collective-permute-done.4.refs_9_), channel_id=1, source_target_pairs={{0,4},{4,0},{8,12},{12,8},{16,20},{20,16},{24,28},{28,24},{1,5},{5... | collective-permute-start | bytes 417800 | tf_op jit(solution)/shard_map/ppermute | solution.py:411
  23.8 10.7 %copy-start = (f32[512]{0:T(512)S(1)}, f32[512]{0:T(512)}, u32[]{:S(2)}) copy-start(f32[512]{0:T(512)} %param.13) | copy-start | bytes 6148
  29.8 1.9 %collective-permute-start.7 = (f32[1,512]{1,0:T(1,128)S(1)}, f32[1,512]{1,0:T(1,128)S(1)}, u32[]{:S(2)}, u32[]{:S(2)}) collective-permute-start(f32[1,512]{1,0:T(1,128)S(1)} %get-tuple-element.32.refs_3_), channel_id=1, source_target_pairs={{0,1},{1,0},{2,3},{3,2},{4,5},{5,4},{6,7},{7,6},{8,9},{9,8},{10,11... | collective-permute-start | bytes 6152 | tf_op jit(solution)/shard_map/ppermute | solution.py:505
  29.9 3.7 %collective-permute-start.8 = (f32[1,512]{1,0:T(1,128)S(1)}, f32[1,512]{1,0:T(1,128)S(1)}, u32[]{:S(2)}, u32[]{:S(2)}) collective-permute-start(f32[1,512]{1,0:T(1,128)S(1)} %get-tuple-element.32.refs_3_), channel_id=1, source_target_pairs={{0,2},{1,3},{2,0},{3,1},{4,6},{5,7},{6,4},{7,5},{8,10},{9,11},{10,... | collective-permute-start | bytes 6152 | tf_op jit(solution)/shard_map/ppermute | solution.py:505
  31.5 3.0 %collective-permute-start.9 = (f32[1,512]{1,0:T(1,128)S(1)}, f32[1,512]{1,0:T(1,128)S(1)}, u32[]{:S(2)}, u32[]{:S(2)}) collective-permute-start(f32[1,512]{1,0:T(1,128)S(1)} %get-tuple-element.32.refs_3_), channel_id=1, source_target_pairs={{0,3},{1,2},{2,1},{3,0},{4,7},{5,6},{6,5},{7,4},{8,11},{9,10},{10,... | collective-permute-start | bytes 6152 | tf_op jit(solution)/shard_map/ppermute | solution.py:505
  36.2 6.0 %collective-permute-start.11 = (bf16[8,16,256]{2,1,0:T(8,128)(2,1)S(1)}, bf16[8,16,256]{2,1,0:T(8,128)(2,1)S(1)}, u32[]{:S(2)}, u32[]{:S(2)}) collective-permute-start(bf16[8,16,256]{2,1,0:T(8,128)(2,1)S(1)} %get-tuple-element.36), channel_id=1, source_target_pairs={{0,8},{4,12},{8,0},{12,4},{16,24},{20,28},{24,16},{28,20},{1,9},{5... | collective-permute-start | bytes 196616 | tf_op jit(solution)/shard_map/ppermute | solution.py:411
  37.6 8.2 %collective-permute-start.13 = (bf16[8,16,256]{2,1,0:T(8,128)(2,1)S(1)}, bf16[8,16,256]{2,1,0:T(8,128)(2,1)S(1)}, u32[]{:S(2)}, u32[]{:S(2)}) collective-permute-start(bf16[8,16,256]{2,1,0:T(8,128)(2,1)S(1)} %get-tuple-element.36), channel_id=1, source_target_pairs={{0,16},{4,20},{8,24},{12,28},{16,0},{20,4},{24,8},{28,12},{1,17},{... | collective-permute-start | bytes 196616 | tf_op jit(solution)/shard_map/ppermute | solution.py:411
  39.3 7.8 %collective-permute-start.15 = (bf16[8,16,256]{2,1,0:T(8,128)(2,1)S(1)}, bf16[8,16,256]{2,1,0:T(8,128)(2,1)S(1)}, u32[]{:S(2)}, u32[]{:S(2)}) collective-permute-start(bf16[8,16,256]{2,1,0:T(8,128)(2,1)S(1)} %get-tuple-element.36), channel_id=1, source_target_pairs={{0,24},{4,28},{8,16},{12,20},{16,8},{20,12},{24,0},{28,4},{1,25},{... | collective-permute-start | bytes 196616 | tf_op jit(solution)/shard_map/ppermute | solution.py:411
  40.7 7.2 %collective-permute-start.10 = (bf16[8,16,256]{2,1,0:T(8,128)(2,1)S(1)}, bf16[8,16,256]{2,1,0:T(8,128)(2,1)S(1)}, u32[]{:S(2)}, u32[]{:S(2)}) collective-permute-start(bf16[8,16,256]{2,1,0:T(8,128)(2,1)S(1)} %get-tuple-element.36), channel_id=1, source_target_pairs={{0,4},{4,0},{8,12},{12,8},{16,20},{20,16},{24,28},{28,24},{1,5},{5... | collective-permute-start | bytes 196616 | tf_op jit(solution)/shard_map/ppermute | solution.py:411
  42.3 5.6 %collective-permute-start.12 = (bf16[8,16,256]{2,1,0:T(8,128)(2,1)S(1)}, bf16[8,16,256]{2,1,0:T(8,128)(2,1)S(1)}, u32[]{:S(2)}, u32[]{:S(2)}) collective-permute-start(bf16[8,16,256]{2,1,0:T(8,128)(2,1)S(1)} %collective-permute-done.11.refs_9_), channel_id=1, source_target_pairs={{0,4},{4,0},{8,12},{12,8},{16,20},{20,16},{24,28},{28,24},{1,5},{5... | collective-permute-start | bytes 196616 | tf_op jit(solution)/shard_map/ppermute | solution.py:411
  45.8 4.3 %collective-permute-start.14 = (bf16[8,16,256]{2,1,0:T(8,128)(2,1)S(1)}, bf16[8,16,256]{2,1,0:T(8,128)(2,1)S(1)}, u32[]{:S(2)}, u32[]{:S(2)}) collective-permute-start(bf16[8,16,256]{2,1,0:T(8,128)(2,1)S(1)} %collective-permute-done.13.refs_11_), channel_id=1, source_target_pairs={{0,4},{4,0},{8,12},{12,8},{16,20},{20,16},{24,28},{28,24},{1,5},{5... | collective-permute-start | bytes 196616 | tf_op jit(solution)/shard_map/ppermute | solution.py:411
  47.1 4.3 %collective-permute-start.16 = (bf16[8,16,256]{2,1,0:T(8,128)(2,1)S(1)}, bf16[8,16,256]{2,1,0:T(8,128)(2,1)S(1)}, u32[]{:S(2)}, u32[]{:S(2)}) collective-permute-start(bf16[8,16,256]{2,1,0:T(8,128)(2,1)S(1)} %collective-permute-done.15.refs_13_), channel_id=1, source_target_pairs={{0,4},{4,0},{8,12},{12,8},{16,20},{20,16},{24,28},{28,24},{1,5},{5... | collective-permute-start | bytes 196616 | tf_op jit(solution)/shard_map/ppermute | solution.py:411
  52.7 1.9 %collective-permute-start.17 = (f32[1,512]{1,0:T(1,128)S(1)}, f32[1,512]{1,0:T(1,128)S(1)}, u32[]{:S(2)}, u32[]{:S(2)}) collective-permute-start(f32[1,512]{1,0:T(1,128)S(1)} %get-tuple-element.38.refs_2_), channel_id=1, source_target_pairs={{0,1},{1,0},{2,3},{3,2},{4,5},{5,4},{6,7},{7,6},{8,9},{9,8},{10,11... | collective-permute-start | bytes 6152 | tf_op jit(solution)/shard_map/ppermute | solution.py:505
  52.8 3.7 %collective-permute-start.18 = (f32[1,512]{1,0:T(1,128)S(1)}, f32[1,512]{1,0:T(1,128)S(1)}, u32[]{:S(2)}, u32[]{:S(2)}) collective-permute-start(f32[1,512]{1,0:T(1,128)S(1)} %get-tuple-element.38.refs_2_), channel_id=1, source_target_pairs={{0,2},{1,3},{2,0},{3,1},{4,6},{5,7},{6,4},{7,5},{8,10},{9,11},{10,... | collective-permute-start | bytes 6152 | tf_op jit(solution)/shard_map/ppermute | solution.py:505
  53.4 3.0 %collective-permute-start.19 = (f32[1,512]{1,0:T(1,128)S(1)}, f32[1,512]{1,0:T(1,128)S(1)}, u32[]{:S(2)}, u32[]{:S(2)}) collective-permute-start(f32[1,512]{1,0:T(1,128)S(1)} %get-tuple-element.38.refs_2_), channel_id=1, source_target_pairs={{0,3},{1,2},{2,1},{3,0},{4,7},{5,6},{6,5},{7,4},{8,11},{9,10},{10,... | collective-permute-start | bytes 6152 | tf_op jit(solution)/shard_map/ppermute | solution.py:505
where the time goes:
time: 57.2 us; the launch traced here: 57.1 us
  starting transfers between devices  23.5 us (41%)
  waiting for transfers between devices  19.1 us (33%)
  Pallas kernels  13.1 us (23%)
  between operations  1.41 us (2%)
    ppermute x14, starting transfers between devices, swap(): return lax.ppermute(value, 'scan', [(i, i ^ k) for i in range(count)])  19.7 us
    ppermute x14, waiting for transfers between devices, swap(): return lax.ppermute(value, 'scan', [(i, i ^ k) for i in range(count)])  14.5 us
    ppermute x6, waiting for transfers between devices, body(): lax.ppermute(energy, 'bin', partners(groups, k))  4.55 us
    pallas_call x1, Pallas kernels, body(): pl.pallas_call(functools.partial(start_kernel, coded, columns), out_shape...  3.9 us
    ppermute x6, starting transfers between devices, body(): lax.ppermute(energy, 'bin', partners(groups, k))  3.84 us
    pallas_call x1, Pallas kernels, body(): pl.pallas_call(functools.partial(early_kernel, coded, early), out_shape=(...  3.37 us
    pallas_call x1, Pallas kernels, body(): pl.pallas_call(functools.partial(late_kernel, late, snaps), out_shape=(ma...  2.15 us
    pallas_call x1, Pallas kernels, body(): pl.pallas_call(functools.partial(next_kernel, groups, snaps), out_shape=(...  1.75 us
  transfers between devices with their start and end apart: 20, of which 9 were waited for; matrix products, arithmetic and copies ran while one was open for 0% of the time, Pallas kernels for 6%

commit v1 on v0

--- a/solution.py
+++ b/solution.py
@@ -501,10 +501,9 @@
                 scratch_shapes=[pltpu.VMEM(slot_shape.shape, F32)],
                 compiler_params=grant,
             )(info, step_size, entries, more, contrib, current, chosen, held, *received)
-        energies = [energy] + [
-            lax.ppermute(energy, "bin", partners(groups, k))
-            for k in range(1, groups)
-        ]
+        energies = [energy]
+        for k in range(1, groups):
+            energies.append(lax.ppermute(energy, "bin", partners(groups, k)))
         if iteration < ITERS - 1:
             current, contrib, sent = pl.pallas_call(
                 functools.partial(next_kernel, groups, snaps),

time: 57.2 us -> 57.2 us (level)
  no operation moved by 1% of the time
where the time goes in v1:
time: 57.2 us; the launch traced here: 57.1 us
  starting transfers between devices  23.5 us (41%)
  waiting for transfers between devices  19.1 us (33%)
  Pallas kernels  13.1 us (23%)
  between operations  1.41 us (2%)
    ppermute x14, starting transfers between devices, swap(): return lax.ppermute(value, 'scan', [(i, i ^ k) for i in range(count)])  19.7 us
    ppermute x14, waiting for transfers between devices, swap(): return lax.ppermute(value, 'scan', [(i, i ^ k) for i in range(count)])  14.5 us
    ppermute x6, waiting for transfers between devices, body(): energies.append(lax.ppermute(energy, 'bin', partners(groups, k)))  4.55 us
    pallas_call x1, Pallas kernels, body(): pl.pallas_call(functools.partial(start_kernel, coded, columns), out_shape...  3.9 us
    ppermute x6, starting transfers between devices, body(): energies.append(lax.ppermute(energy, 'bin', partners(groups, k)))  3.84 us
    pallas_call x1, Pallas kernels, body(): pl.pallas_call(functools.partial(early_kernel, coded, early), out_shape=(...  3.37 us
    pallas_call x1, Pallas kernels, body(): pl.pallas_call(functools.partial(late_kernel, late, snaps), out_shape=(ma...  2.15 us
    pallas_call x1, Pallas kernels, body(): pl.pallas_call(functools.partial(next_kernel, groups, snaps), out_shape=(...  1.75 us
  transfers between devices with their start and end apart: 20, of which 9 were waited for; matrix products, arithmetic and copies ran while one was open for 0% of the time, Pallas kernels for 6%

profile of v1, /device:TPU:0, one launch (start us, length us, event | category | flops | bytes accessed | tf_op | source)
XLA Modules:
  0.0 57.1 jit_solution(13967366978907937359)
XLA Ops:
  0.7 3.9 %shard_map.73 = (f32[16,512]{1,0:T(8,128)S(1)}, f32[8,16,256]{2,1,0:T(8,128)S(1)}, s16[17,16,256]{2,1,0:T(8,128)(2,1)S(1)}, s32[26]{0:T(128)S(1)}) custom-call(s32[1]{0:T(128)S(6)} %copy.8.count_ref, s32[2,8]{1,0:T(2,128)} %pattern_hbm.1, f32[4,4,512]{2,1,0:T(4,128)} %x_hbm.1, f32[4,4,2048]{2,1,0:T(4,128)} %m_hbm.1, bf16[8,4,256,256]{3,2,1,0:T(8,128)(2,1)} %refs_3_.1), custom_call_target="tpu_custom_call" | custom-call | tf_op jit(solution)/shard_map/pallas_call | solution.py:424
  4.6 3.1 %collective-permute-start.1 = (s16[17,16,256]{2,1,0:T(8,128)(2,1)S(1)}, s16[17,16,256]{2,1,0:T(8,128)(2,1)S(1)}, u32[]{:S(2)}, u32[]{:S(2)}) collective-permute-start(s16[17,16,256]{2,1,0:T(8,128)(2,1)S(1)} %get-tuple-element.24.refs_4_), channel_id=1, source_target_pairs={{0,8},{4,12},{8,0},{12,4},{16,24},{20,28},{24,16},{28,20},{1,9},{5... | collective-permute-start | bytes 417800 | tf_op jit(solution)/shard_map/ppermute | solution.py:411
  7.7 2.6 %collective-permute-start.3 = (s16[17,16,256]{2,1,0:T(8,128)(2,1)S(1)}, s16[17,16,256]{2,1,0:T(8,128)(2,1)S(1)}, u32[]{:S(2)}, u32[]{:S(2)}) collective-permute-start(s16[17,16,256]{2,1,0:T(8,128)(2,1)S(1)} %get-tuple-element.24.refs_4_), channel_id=1, source_target_pairs={{0,16},{4,20},{8,24},{12,28},{16,0},{20,4},{24,8},{28,12},{1,17},{... | collective-permute-start | bytes 417800 | tf_op jit(solution)/shard_map/ppermute | solution.py:411
  10.3 1.7 %collective-permute-start = (s16[17,16,256]{2,1,0:T(8,128)(2,1)S(1)}, s16[17,16,256]{2,1,0:T(8,128)(2,1)S(1)}, u32[]{:S(2)}, u32[]{:S(2)}) collective-permute-start(s16[17,16,256]{2,1,0:T(8,128)(2,1)S(1)} %get-tuple-element.24.refs_4_), channel_id=1, source_target_pairs={{0,4},{4,0},{8,12},{12,8},{16,20},{20,16},{24,28},{28,24},{1,5},{5... | collective-permute-start | bytes 417800 | tf_op jit(solution)/shard_map/ppermute | solution.py:411
  12.0 1.2 %collective-permute-done.1.refs_6_ = s16[17,16,256]{2,1,0:T(8,128)(2,1)S(1)} collective-permute-done((s16[17,16,256]{2,1,0:T(8,128)(2,1)S(1)}, s16[17,16,256]{2,1,0:T(8,128)(2,1)S(1)}, u32[]{:S(2)}, u32[]{:S(2)}) %collective-permute-start.1) | collective-permute-done | bytes 139296 | tf_op jit(solution)/shard_map/ppermute | solution.py:411
  13.2 1.7 %collective-permute-start.2 = (s16[17,16,256]{2,1,0:T(8,128)(2,1)S(1)}, s16[17,16,256]{2,1,0:T(8,128)(2,1)S(1)}, u32[]{:S(2)}, u32[]{:S(2)}) collective-permute-start(s16[17,16,256]{2,1,0:T(8,128)(2,1)S(1)} %collective-permute-done.1.refs_6_), channel_id=1, source_target_pairs={{0,4},{4,0},{8,12},{12,8},{16,20},{20,16},{24,28},{28,24},{1,5},{5... | collective-permute-start | bytes 417800 | tf_op jit(solution)/shard_map/ppermute | solution.py:411
  14.9 6.2 %collective-permute-done.3.refs_8_ = s16[17,16,256]{2,1,0:T(8,128)(2,1)S(1)} collective-permute-done((s16[17,16,256]{2,1,0:T(8,128)(2,1)S(1)}, s16[17,16,256]{2,1,0:T(8,128)(2,1)S(1)}, u32[]{:S(2)}, u32[]{:S(2)}) %collective-permute-start.3) | collective-permute-done | bytes 139296 | tf_op jit(solution)/shard_map/ppermute | solution.py:411
  21.1 1.5 %collective-permute-start.5 = (s16[17,16,256]{2,1,0:T(8,128)(2,1)S(1)}, s16[17,16,256]{2,1,0:T(8,128)(2,1)S(1)}, u32[]{:S(2)}, u32[]{:S(2)}) collective-permute-start(s16[17,16,256]{2,1,0:T(8,128)(2,1)S(1)} %collective-permute-done.3.refs_8_), channel_id=1, source_target_pairs={{0,4},{4,0},{8,12},{12,8},{16,20},{20,16},{24,28},{28,24},{1,5},{5... | collective-permute-start | bytes 417800 | tf_op jit(solution)/shard_map/ppermute | solution.py:411
  23.8 3.4 %shard_map.74 = (f32[8,16,256]{2,1,0:T(8,128)S(1)}, f32[8,16,256]{2,1,0:T(8,128)S(1)}, bf16[8,4,256,256]{3,2,1,0:T(8,128)(2,1)S(1)}, s32[56]{0:T(128)S(1)}) custom-call(s32[26]{0:T(128)S(1)} %get-tuple-element.22.refs_0_, s32[1]{0:T(128)} %bitcast.refs_1_.refs_2_, f32[8,16,256]{2,1,0:T(8,128)S(1)} %get-tuple-element.23.refs_2_, ...), custom_call_target="tpu_custom_call" | custom-call | tf_op jit(solution)/shard_map/pallas_call | solution.py:478
  27.6 2.1 %shard_map.75 = (f32[16,512]{1,0:T(8,128)S(1)}, f32[1,512]{1,0:T(1,128)S(1)}, f32[8,16,256]{2,1,0:T(8,128)S(1)}, s32[20]{0:T(128)S(1)}) custom-call(s32[26]{0:T(128)S(1)} %get-tuple-element.22.refs_0_, f32[1]{0:T(128)S(6)} %copy.9.refs_1_.refs_0_, s32[1]{0:T(128)} %bitcast.refs_1_.refs_2_, f32[8,16,256]{2,1,0:T(8,128)S(1)} %get-tuple-element.26.refs_3_, ...), custom_call_target="tpu_custom_call" | custom-call | tf_op jit(solution)/shard_map/pallas_call | solution.py:486
  29.9 1.6 %collective-permute-start.8 = (f32[1,512]{1,0:T(1,128)S(1)}, f32[1,512]{1,0:T(1,128)S(1)}, u32[]{:S(2)}, u32[]{:S(2)}) collective-permute-start(f32[1,512]{1,0:T(1,128)S(1)} %get-tuple-element.32.refs_3_), channel_id=1, source_target_pairs={{0,2},{1,3},{2,0},{3,1},{4,6},{5,7},{6,4},{7,5},{8,10},{9,11},{10,... | collective-permute-start | bytes 6152 | tf_op jit(solution)/shard_map/ppermute | solution.py:506
  31.7 1.8 %collective-permute-done.8.refs_5_ = f32[1,512]{1,0:T(1,128)S(1)} collective-permute-done((f32[1,512]{1,0:T(1,128)S(1)}, f32[1,512]{1,0:T(1,128)S(1)}, u32[]{:S(2)}, u32[]{:S(2)}) %collective-permute-start.8) | collective-permute-done | bytes 2080 | tf_op jit(solution)/shard_map/ppermute | solution.py:506
  34.5 1.7 %shard_map.76 = (f32[16,512]{1,0:T(8,128)S(1)}, f32[8,16,256]{2,1,0:T(8,128)S(1)}, bf16[8,16,256]{2,1,0:T(8,128)(2,1)S(1)}) custom-call(s32[26]{0:T(128)S(1)} %get-tuple-element.22.refs_0_, f32[1]{0:T(128)S(6)} %copy.9.refs_1_.refs_0_, f32[16,512]{1,0:T(8,128)S(1)} %get-tuple-element.31.refs_2_, f32[1,512]{1,0:T(1,128)S(1)} %get-tuple-element.32.refs_3_, ...), custom_call_target="tpu_custom_call" | custom-call | tf_op jit(solution)/shard_map/pallas_call | solution.py:508
  36.2 1.4 %collective-permute-start.11 = (bf16[8,16,256]{2,1,0:T(8,128)(2,1)S(1)}, bf16[8,16,256]{2,1,0:T(8,128)(2,1)S(1)}, u32[]{:S(2)}, u32[]{:S(2)}) collective-permute-start(bf16[8,16,256]{2,1,0:T(8,128)(2,1)S(1)} %get-tuple-element.36), channel_id=1, source_target_pairs={{0,8},{4,12},{8,0},{12,4},{16,24},{20,28},{24,16},{28,20},{1,9},{5... | collective-permute-start | bytes 196616 | tf_op jit(solution)/shard_map/ppermute | solution.py:411
  37.6 1.7 %collective-permute-start.13 = (bf16[8,16,256]{2,1,0:T(8,128)(2,1)S(1)}, bf16[8,16,256]{2,1,0:T(8,128)(2,1)S(1)}, u32[]{:S(2)}, u32[]{:S(2)}) collective-permute-start(bf16[8,16,256]{2,1,0:T(8,128)(2,1)S(1)} %get-tuple-element.36), channel_id=1, source_target_pairs={{0,16},{4,20},{8,24},{12,28},{16,0},{20,4},{24,8},{28,12},{1,17},{... | collective-permute-start | bytes 196616 | tf_op jit(solution)/shard_map/ppermute | solution.py:411
  39.3 1.3 %collective-permute-start.15 = (bf16[8,16,256]{2,1,0:T(8,128)(2,1)S(1)}, bf16[8,16,256]{2,1,0:T(8,128)(2,1)S(1)}, u32[]{:S(2)}, u32[]{:S(2)}) collective-permute-start(bf16[8,16,256]{2,1,0:T(8,128)(2,1)S(1)} %get-tuple-element.36), channel_id=1, source_target_pairs={{0,24},{4,28},{8,16},{12,20},{16,8},{20,12},{24,0},{28,4},{1,25},{... | collective-permute-start | bytes 196616 | tf_op jit(solution)/shard_map/ppermute | solution.py:411
  40.7 1.6 %collective-permute-start.10 = (bf16[8,16,256]{2,1,0:T(8,128)(2,1)S(1)}, bf16[8,16,256]{2,1,0:T(8,128)(2,1)S(1)}, u32[]{:S(2)}, u32[]{:S(2)}) collective-permute-start(bf16[8,16,256]{2,1,0:T(8,128)(2,1)S(1)} %get-tuple-element.36), channel_id=1, source_target_pairs={{0,4},{4,0},{8,12},{12,8},{16,20},{20,16},{24,28},{28,24},{1,5},{5... | collective-permute-start | bytes 196616 | tf_op jit(solution)/shard_map/ppermute | solution.py:411
  42.7 3.1 %collective-permute-done.13.refs_11_ = bf16[8,16,256]{2,1,0:T(8,128)(2,1)S(1)} collective-permute-done((bf16[8,16,256]{2,1,0:T(8,128)(2,1)S(1)}, bf16[8,16,256]{2,1,0:T(8,128)(2,1)S(1)}, u32[]{:S(2)}, u32[]{:S(2)}) %collective-permute-start.13) | collective-permute-done | bytes 65568 | tf_op jit(solution)/shard_map/ppermute | solution.py:411
  45.8 1.3 %collective-permute-start.14 = (bf16[8,16,256]{2,1,0:T(8,128)(2,1)S(1)}, bf16[8,16,256]{2,1,0:T(8,128)(2,1)S(1)}, u32[]{:S(2)}, u32[]{:S(2)}) collective-permute-start(bf16[8,16,256]{2,1,0:T(8,128)(2,1)S(1)} %collective-permute-done.13.refs_11_), channel_id=1, source_target_pairs={{0,4},{4,0},{8,12},{12,8},{16,20},{20,16},{24,28},{28,24},{1,5},{5... | collective-permute-start | bytes 196616 | tf_op jit(solution)/shard_map/ppermute | solution.py:411
  47.9 2.2 %collective-permute-done.14.refs_12_ = bf16[8,16,256]{2,1,0:T(8,128)(2,1)S(1)} collective-permute-done((bf16[8,16,256]{2,1,0:T(8,128)(2,1)S(1)}, bf16[8,16,256]{2,1,0:T(8,128)(2,1)S(1)}, u32[]{:S(2)}, u32[]{:S(2)}) %collective-permute-start.14) | collective-permute-done | bytes 65568 | tf_op jit(solution)/shard_map/ppermute | solution.py:411
  50.1 1.3 %collective-permute-done.16.refs_14_ = bf16[8,16,256]{2,1,0:T(8,128)(2,1)S(1)} collective-permute-done((bf16[8,16,256]{2,1,0:T(8,128)(2,1)S(1)}, bf16[8,16,256]{2,1,0:T(8,128)(2,1)S(1)}, u32[]{:S(2)}, u32[]{:S(2)}) %collective-permute-start.16) | collective-permute-done | bytes 65568 | tf_op jit(solution)/shard_map/ppermute | solution.py:411
  51.4 1.3 %shard_map.77 = (f32[16,512]{1,0:T(8,128)S(1)}, f32[1,512]{1,0:T(1,128)S(1)}) custom-call(s32[26]{0:T(128)S(1)} %get-tuple-element.22.refs_0_, f32[1]{0:T(128)S(6)} %copy.9.refs_1_.refs_0_, s32[56]{0:T(128)S(1)} %get-tuple-element.25.refs_2_, s32[20]{0:T(128)S(1)} %get-tuple-element.30.refs_3_, f32[8,16,256]{2,1,0:T(8,128)S(1)} %get-tuple-element.33.refs_4_, ...), custom_call_target="tpu_custom_call" | custom-call | tf_op jit(solution)/shard_map/pallas_call | solution.py:496
  53.4 1.2 %collective-permute-start.19 = (f32[1,512]{1,0:T(1,128)S(1)}, f32[1,512]{1,0:T(1,128)S(1)}, u32[]{:S(2)}, u32[]{:S(2)}) collective-permute-start(f32[1,512]{1,0:T(1,128)S(1)} %get-tuple-element.38.refs_2_), channel_id=1, source_target_pairs={{0,3},{1,2},{2,1},{3,0},{4,7},{5,6},{6,5},{7,4},{8,11},{9,10},{10,... | collective-permute-start | bytes 6152 | tf_op jit(solution)/shard_map/ppermute | solution.py:506
  54.6 1.8 %collective-permute-done.18.refs_4_ = f32[1,512]{1,0:T(1,128)S(1)} collective-permute-done((f32[1,512]{1,0:T(1,128)S(1)}, f32[1,512]{1,0:T(1,128)S(1)}, u32[]{:S(2)}, u32[]{:S(2)}) %collective-permute-start.18) | collective-permute-done | bytes 2080 | tf_op jit(solution)/shard_map/ppermute | solution.py:506
  (24 shorter events, 4.8 us)
Async XLA Ops:
  4.6 8.6 %collective-permute-start.1 = (s16[17,16,256]{2,1,0:T(8,128)(2,1)S(1)}, s16[17,16,256]{2,1,0:T(8,128)(2,1)S(1)}, u32[]{:S(2)}, u32[]{:S(2)}) collective-permute-start(s16[17,16,256]{2,1,0:T(8,128)(2,1)S(1)} %get-tuple-element.24.refs_4_), channel_id=1, source_target_pairs={{0,8},{4,12},{8,0},{12,4},{16,24},{20,28},{24,16},{28,20},{1,9},{5... | collective-permute-start | bytes 417800 | tf_op jit(solution)/shard_map/ppermute | solution.py:411
  7.7 13.4 %collective-permute-start.3 = (s16[17,16,256]{2,1,0:T(8,128)(2,1)S(1)}, s16[17,16,256]{2,1,0:T(8,128)(2,1)S(1)}, u32[]{:S(2)}, u32[]{:S(2)}) collective-permute-start(s16[17,16,256]{2,1,0:T(8,128)(2,1)S(1)} %get-tuple-element.24.refs_4_), channel_id=1, source_target_pairs={{0,16},{4,20},{8,24},{12,28},{16,0},{20,4},{24,8},{28,12},{1,17},{... | collective-permute-start | bytes 417800 | tf_op jit(solution)/shard_map/ppermute | solution.py:411
  10.3 12.3 %collective-permute-start.4 = (s16[17,16,256]{2,1,0:T(8,128)(2,1)S(1)}, s16[17,16,256]{2,1,0:T(8,128)(2,1)S(1)}, u32[]{:S(2)}, u32[]{:S(2)}) collective-permute-start(s16[17,16,256]{2,1,0:T(8,128)(2,1)S(1)} %get-tuple-element.24.refs_4_), channel_id=1, source_target_pairs={{0,24},{4,28},{8,16},{12,20},{16,8},{20,12},{24,0},{28,4},{1,25},{... | collective-permute-start | bytes 417800 | tf_op jit(solution)/shard_map/ppermute | solution.py:411
  10.3 13.5 %collective-permute-start = (s16[17,16,256]{2,1,0:T(8,128)(2,1)S(1)}, s16[17,16,256]{2,1,0:T(8,128)(2,1)S(1)}, u32[]{:S(2)}, u32[]{:S(2)}) collective-permute-start(s16[17,16,256]{2,1,0:T(8,128)(2,1)S(1)} %get-tuple-element.24.refs_4_), channel_id=1, source_target_pairs={{0,4},{4,0},{8,12},{12,8},{16,20},{20,16},{24,28},{28,24},{1,5},{5... | collective-permute-start | bytes 417800 | tf_op jit(solution)/shard_map/ppermute | solution.py:411
  13.2 10.6 %collective-permute-start.2 = (s16[17,16,256]{2,1,0:T(8,128)(2,1)S(1)}, s16[17,16,256]{2,1,0:T(8,128)(2,1)S(1)}, u32[]{:S(2)}, u32[]{:S(2)}) collective-permute-start(s16[17,16,256]{2,1,0:T(8,128)(2,1)S(1)} %collective-permute-done.1.refs_6_), channel_id=1, source_target_pairs={{0,4},{4,0},{8,12},{12,8},{16,20},{20,16},{24,28},{28,24},{1,5},{5... | collective-permute-start | bytes 417800 | tf_op jit(solution)/shard_map/ppermute | solution.py:411
  21.1 6.1 %collective-permute-start.5 = (s16[17,16,256]{2,1,0:T(8,128)(2,1)S(1)}, s16[17,16,256]{2,1,0:T(8,128)(2,1)S(1)}, u32[]{:S(2)}, u32[]{:S(2)}) collective-permute-start(s16[17,16,256]{2,1,0:T(8,128)(2,1)S(1)} %collective-permute-done.3.refs_8_), channel_id=1, source_target_pairs={{0,4},{4,0},{8,12},{12,8},{16,20},{20,16},{24,28},{28,24},{1,5},{5... | collective-permute-start | bytes 417800 | tf_op jit(solution)/shard_map/ppermute | solution.py:411
  22.6 5.1 %collective-permute-start.6 = (s16[17,16,256]{2,1,0:T(8,128)(2,1)S(1)}, s16[17,16,256]{2,1,0:T(8,128)(2,1)S(1)}, u32[]{:S(2)}, u32[]{:S(2)}) collective-permute-start(s16[17,16,256]{2,1,0:T(8,128)(2,1)S(1)} %collective-permute-done.4.refs_9_), channel_id=1, source_target_pairs={{0,4},{4,0},{8,12},{12,8},{16,20},{20,16},{24,28},{28,24},{1,5},{5... | collective-permute-start | bytes 417800 | tf_op jit(solution)/shard_map/ppermute | solution.py:411
  23.8 10.7 %copy-start = (f32[512]{0:T(512)S(1)}, f32[512]{0:T(512)}, u32[]{:S(2)}) copy-start(f32[512]{0:T(512)} %param.13) | copy-start | bytes 6148
  29.8 1.9 %collective-permute-start.7 = (f32[1,512]{1,0:T(1,128)S(1)}, f32[1,512]{1,0:T(1,128)S(1)}, u32[]{:S(2)}, u32[]{:S(2)}) collective-permute-start(f32[1,512]{1,0:T(1,128)S(1)} %get-tuple-element.32.refs_3_), channel_id=1, source_target_pairs={{0,1},{1,0},{2,3},{3,2},{4,5},{5,4},{6,7},{7,6},{8,9},{9,8},{10,11... | collective-permute-start | bytes 6152 | tf_op jit(solution)/shard_map/ppermute | solution.py:506
  29.9 3.7 %collective-permute-start.8 = (f32[1,512]{1,0:T(1,128)S(1)}, f32[1,512]{1,0:T(1,128)S(1)}, u32[]{:S(2)}, u32[]{:S(2)}) collective-permute-start(f32[1,512]{1,0:T(1,128)S(1)} %get-tuple-element.32.refs_3_), channel_id=1, source_target_pairs={{0,2},{1,3},{2,0},{3,1},{4,6},{5,7},{6,4},{7,5},{8,10},{9,11},{10,... | collective-permute-start | bytes 6152 | tf_op jit(solution)/shard_map/ppermute | solution.py:506
  31.5 3.0 %collective-permute-start.9 = (f32[1,512]{1,0:T(1,128)S(1)}, f32[1,512]{1,0:T(1,128)S(1)}, u32[]{:S(2)}, u32[]{:S(2)}) collective-permute-start(f32[1,512]{1,0:T(1,128)S(1)} %get-tuple-element.32.refs_3_), channel_id=1, source_target_pairs={{0,3},{1,2},{2,1},{3,0},{4,7},{5,6},{6,5},{7,4},{8,11},{9,10},{10,... | collective-permute-start | bytes 6152 | tf_op jit(solution)/shard_map/ppermute | solution.py:506
  36.2 6.0 %collective-permute-start.11 = (bf16[8,16,256]{2,1,0:T(8,128)(2,1)S(1)}, bf16[8,16,256]{2,1,0:T(8,128)(2,1)S(1)}, u32[]{:S(2)}, u32[]{:S(2)}) collective-permute-start(bf16[8,16,256]{2,1,0:T(8,128)(2,1)S(1)} %get-tuple-element.36), channel_id=1, source_target_pairs={{0,8},{4,12},{8,0},{12,4},{16,24},{20,28},{24,16},{28,20},{1,9},{5... | collective-permute-start | bytes 196616 | tf_op jit(solution)/shard_map/ppermute | solution.py:411
  37.6 8.2 %collective-permute-start.13 = (bf16[8,16,256]{2,1,0:T(8,128)(2,1)S(1)}, bf16[8,16,256]{2,1,0:T(8,128)(2,1)S(1)}, u32[]{:S(2)}, u32[]{:S(2)}) collective-permute-start(bf16[8,16,256]{2,1,0:T(8,128)(2,1)S(1)} %get-tuple-element.36), channel_id=1, source_target_pairs={{0,16},{4,20},{8,24},{12,28},{16,0},{20,4},{24,8},{28,12},{1,17},{... | collective-permute-start | bytes 196616 | tf_op jit(solution)/shard_map/ppermute | solution.py:411
  39.3 7.8 %collective-permute-start.15 = (bf16[8,16,256]{2,1,0:T(8,128)(2,1)S(1)}, bf16[8,16,256]{2,1,0:T(8,128)(2,1)S(1)}, u32[]{:S(2)}, u32[]{:S(2)}) collective-permute-start(bf16[8,16,256]{2,1,0:T(8,128)(2,1)S(1)} %get-tuple-element.36), channel_id=1, source_target_pairs={{0,24},{4,28},{8,16},{12,20},{16,8},{20,12},{24,0},{28,4},{1,25},{... | collective-permute-start | bytes 196616 | tf_op jit(solution)/shard_map/ppermute | solution.py:411
  40.7 7.2 %collective-permute-start.10 = (bf16[8,16,256]{2,1,0:T(8,128)(2,1)S(1)}, bf16[8,16,256]{2,1,0:T(8,128)(2,1)S(1)}, u32[]{:S(2)}, u32[]{:S(2)}) collective-permute-start(bf16[8,16,256]{2,1,0:T(8,128)(2,1)S(1)} %get-tuple-element.36), channel_id=1, source_target_pairs={{0,4},{4,0},{8,12},{12,8},{16,20},{20,16},{24,28},{28,24},{1,5},{5... | collective-permute-start | bytes 196616 | tf_op jit(solution)/shard_map/ppermute | solution.py:411
  42.3 5.6 %collective-permute-start.12 = (bf16[8,16,256]{2,1,0:T(8,128)(2,1)S(1)}, bf16[8,16,256]{2,1,0:T(8,128)(2,1)S(1)}, u32[]{:S(2)}, u32[]{:S(2)}) collective-permute-start(bf16[8,16,256]{2,1,0:T(8,128)(2,1)S(1)} %collective-permute-done.11.refs_9_), channel_id=1, source_target_pairs={{0,4},{4,0},{8,12},{12,8},{16,20},{20,16},{24,28},{28,24},{1,5},{5... | collective-permute-start | bytes 196616 | tf_op jit(solution)/shard_map/ppermute | solution.py:411
  45.8 4.3 %collective-permute-start.14 = (bf16[8,16,256]{2,1,0:T(8,128)(2,1)S(1)}, bf16[8,16,256]{2,1,0:T(8,128)(2,1)S(1)}, u32[]{:S(2)}, u32[]{:S(2)}) collective-permute-start(bf16[8,16,256]{2,1,0:T(8,128)(2,1)S(1)} %collective-permute-done.13.refs_11_), channel_id=1, source_target_pairs={{0,4},{4,0},{8,12},{12,8},{16,20},{20,16},{24,28},{28,24},{1,5},{5... | collective-permute-start | bytes 196616 | tf_op jit(solution)/shard_map/ppermute | solution.py:411
  47.1 4.3 %collective-permute-start.16 = (bf16[8,16,256]{2,1,0:T(8,128)(2,1)S(1)}, bf16[8,16,256]{2,1,0:T(8,128)(2,1)S(1)}, u32[]{:S(2)}, u32[]{:S(2)}) collective-permute-start(bf16[8,16,256]{2,1,0:T(8,128)(2,1)S(1)} %collective-permute-done.15.refs_13_), channel_id=1, source_target_pairs={{0,4},{4,0},{8,12},{12,8},{16,20},{20,16},{24,28},{28,24},{1,5},{5... | collective-permute-start | bytes 196616 | tf_op jit(solution)/shard_map/ppermute | solution.py:411
  52.7 1.9 %collective-permute-start.17 = (f32[1,512]{1,0:T(1,128)S(1)}, f32[1,512]{1,0:T(1,128)S(1)}, u32[]{:S(2)}, u32[]{:S(2)}) collective-permute-start(f32[1,512]{1,0:T(1,128)S(1)} %get-tuple-element.38.refs_2_), channel_id=1, source_target_pairs={{0,1},{1,0},{2,3},{3,2},{4,5},{5,4},{6,7},{7,6},{8,9},{9,8},{10,11... | collective-permute-start | bytes 6152 | tf_op jit(solution)/shard_map/ppermute | solution.py:506
  52.8 3.7 %collective-permute-start.18 = (f32[1,512]{1,0:T(1,128)S(1)}, f32[1,512]{1,0:T(1,128)S(1)}, u32[]{:S(2)}, u32[]{:S(2)}) collective-permute-start(f32[1,512]{1,0:T(1,128)S(1)} %get-tuple-element.38.refs_2_), channel_id=1, source_target_pairs={{0,2},{1,3},{2,0},{3,1},{4,6},{5,7},{6,4},{7,5},{8,10},{9,11},{10,... | collective-permute-start | bytes 6152 | tf_op jit(solution)/shard_map/ppermute | solution.py:506
  53.4 3.0 %collective-permute-start.19 = (f32[1,512]{1,0:T(1,128)S(1)}, f32[1,512]{1,0:T(1,128)S(1)}, u32[]{:S(2)}, u32[]{:S(2)}) collective-permute-start(f32[1,512]{1,0:T(1,128)S(1)} %get-tuple-element.38.refs_2_), channel_id=1, source_target_pairs={{0,3},{1,2},{2,1},{3,0},{4,7},{5,6},{6,5},{7,4},{8,11},{9,10},{10,... | collective-permute-start | bytes 6152 | tf_op jit(solution)/shard_map/ppermute | solution.py:506
